TPU v7x, 128 devices: a whole 4x4x4 slice. The times are simulated.
128 devices in a mesh: ha: 8 (over z, x_hi), wa: 16 (over x_lo, y, core).
Axes of the slice: x: 4 (x_hi: 2, x_lo: 2; x = x_hi * 2 + x_lo), y: 4, z: 4, core: 2. Of those that a mesh axis runs over, the one named last changes fastest.
Arguments:
- queries: bfloat16 [8, 16, 384, 1536], P('ha', 'wa'), may hold values from -15 to 15
- keys_values: bfloat16 [8, 16, 3, 2, 384, 1536], P('ha', 'wa'), may hold values from -9 to 9
- far_offsets: int32 [16, 8, 12, 2], P('wa', 'ha'), may hold values from 0 to 14, all different within a row; in each aligned block of 12 rows (0 to 11, 12 to 23, ..., all dimensions but the last counted through in order) at most 2 rows name the same one
Outputs:
- attended: bfloat16 [8, 16, 384, 1536], P('ha', 'wa')
Inputs may be any that keep to these rules, and one draw needn't show every extreme that they name: `far_offsets`: within the rows of one device (one tile column w, its 1 tile rows, all heads) each offset is named by at most 2 of those rows; each row names 2 different offsets.
All inputs are finite; a program needn't handle non-finite values.
Results may differ from a plain program's by a relative error of at most 0.0048.
Values may be sent and summed in bfloat16 or wider, within the bound.
A program may use at most 320 MiB of HBM per device.

v0:
```python
import jax
import jax.numpy as jnp
from jax import lax
from jax.sharding import Mesh
from jax.sharding import PartitionSpec as P

HEADS = 12
HD = 128
TILE = 384
TT = 3
FAR = 2
WA = ("wa_0", "wa_1", "wa_2")


def with_halo(array, sides, width):
    for axis, dim in sides:
        devices, length = (lax.axis_size(axis), array.shape[dim])
        up = [(i, (i + 1) % devices) for i in range(devices - 1)]
        down = [(j, i) for i, j in up]
        last = lax.slice_in_dim(array, length - width, length, axis=dim)
        first = lax.slice_in_dim(array, 0, width, axis=dim)
        before = lax.ppermute(last, axis, up)
        after = lax.ppermute(first, axis, down)
        array = jnp.concatenate([before, array, after], axis=dim)
    return array


def cut_along(array, dim, devices):
    dims = array.shape
    blocks = array.reshape(*dims[:dim], devices, dims[dim] // devices, *dims[dim + 1 :])
    return jnp.moveaxis(blocks, dim, 0)


def in_order(blocks, dim):
    blocks = jnp.moveaxis(blocks, 0, dim)
    dims = blocks.shape
    return blocks.reshape(*dims[:dim], dims[dim] * dims[dim + 1], *dims[dim + 2 :])


def moved_by_axis(blocks, axes, order):
    dims = [lax.axis_size(a) for a in axes]
    blocks = blocks.reshape(*dims, *blocks.shape[1:])
    for k in order:
        blocks = lax.all_to_all(blocks, axes[k], split_axis=k, concat_axis=k, tiled=True)
    return blocks.reshape(-1, *blocks.shape[len(axes) :])


def two_step_exchange(array, groups, order, split_dim, concat_dim):
    devices = lax.axis_size(groups[0]) * lax.axis_size(groups[1])
    blocks = cut_along(array, split_dim, devices)
    return in_order(moved_by_axis(blocks, groups, order), concat_dim)


def slot_table(offset_block, column, grid_width, capacity):
    flat_offsets = offset_block.reshape(-1)
    owners = (column + 1 + flat_offsets) % grid_width
    request_count = flat_offsets.shape[0]
    onehot = (owners[:, None] == jnp.arange(grid_width, dtype=jnp.int32)[None, :]).astype(jnp.int32)
    before = jnp.cumsum(onehot, axis=0) - onehot
    places = jnp.sum(onehot * before, axis=1)
    tile_codes = jnp.arange(request_count, dtype=jnp.int32) // FAR
    matches = onehot[:, :, None] * (
        places[:, None, None] == jnp.arange(capacity, dtype=jnp.int32)[None, None, :]
    ).astype(jnp.int32)
    wanted_table = jnp.sum(matches * (tile_codes[:, None, None] + 1), axis=0) - 1
    return (owners, places, wanted_table)


def fetch_tiles(kv_heads, wanted_table):
    clipped = jnp.clip(wanted_table, 0, kv_heads.shape[0] * HEADS - 1)
    return kv_heads[clipped // HEADS, :, :, clipped % HEADS, :]


def on_device(queries, keys_values, far_offsets):
    tile_rows = queries.shape[0]
    grid_width = lax.axis_size(WA)
    column = lax.axis_index(WA)
    first_row = lax.axis_index("ha") * tile_rows
    height = lax.axis_size("ha") * tile_rows
    capacity = max(2, 3 * tile_rows * HEADS * FAR // (2 * (grid_width - 1)))
    padded = with_halo(keys_values, (("ha", 0), (WA, 1)), 1)
    kv_heads = keys_values[:, 0, 1].reshape(tile_rows, 2, TILE, HEADS, HD)
    owners, places, wanted_table = slot_table(far_offsets[0], column, grid_width, capacity)
    arrived = two_step_exchange(
        fetch_tiles(
            kv_heads, two_step_exchange(wanted_table, (("wa_0", "wa_1"), "wa_2"), (1, 0), 0, 0)
        ),
        (("wa_0", "wa_1"), "wa_2"),
        (1, 0),
        0,
        0,
    )
    far_kv = arrived[owners, places].reshape(tile_rows, HEADS, FAR, 2, TILE, HD)
    by_head = jnp.moveaxis(far_kv, 1, 0)
    steps_three = jnp.arange(3, dtype=jnp.int32)
    row_pos = first_row + jnp.arange(tile_rows, dtype=jnp.int32)[:, None] + steps_three[None, :] - 1
    row_inside = (row_pos >= 0) & (row_pos < height)
    col_pos = column + steps_three - 1
    col_inside = (col_pos >= 0) & (col_pos < grid_width)
    inside = row_inside[:, :, None] & col_inside[None, None, :]
    key_mask = jnp.concatenate(
        [
            jnp.repeat(inside.reshape(tile_rows, 9), TT * TILE, axis=1),
            jnp.ones((tile_rows, FAR * TILE), dtype=bool),
        ],
        axis=1,
    )[:, None, :]
    query_tiles = queries[:, 0]
    score_scale = 1.0 / HD**0.5

    def one_head(head_item):
        head_index, far_head = head_item
        head_queries = lax.dynamic_slice_in_dim(query_tiles, head_index * HD, HD, 2)
        head_kv = lax.dynamic_slice_in_dim(padded, head_index * HD, HD, 5)
        window = jnp.stack(
            [head_kv[row_step : row_step + tile_rows] for row_step in range(3)], axis=1
        )
        key_tiles = jnp.concatenate(
            [
                window[:, :, :, :, 0].reshape(tile_rows, 9 * TT * TILE, HD),
                far_head[:, :, 0].reshape(tile_rows, FAR * TILE, HD),
            ],
            axis=1,
        )
        value_tiles = jnp.concatenate(
            [
                window[:, :, :, :, 1].reshape(tile_rows, 9 * TT * TILE, HD),
                far_head[:, :, 1].reshape(tile_rows, FAR * TILE, HD),
            ],
            axis=1,
        )
        scores = (
            jnp.einsum("iqd,ikd->iqk", head_queries, key_tiles, preferred_element_type=jnp.float32)
            * score_scale
        )
        scores = jnp.where(key_mask, scores, -1e30)
        peak_score = jnp.max(scores, axis=2, keepdims=True)
        weights = jnp.exp(scores - peak_score)
        totals = jnp.sum(weights, axis=2, keepdims=True)
        summed = jnp.einsum(
            "iqk,ikd->iqd",
            weights.astype(jnp.bfloat16),
            value_tiles,
            preferred_element_type=jnp.float32,
        )
        return (summed / totals).astype(jnp.bfloat16)

    per_head = lax.map(one_head, (jnp.arange(HEADS, dtype=jnp.int32), by_head))
    attended = jnp.transpose(per_head, (1, 2, 0, 3)).reshape(tile_rows, 1, TILE, HEADS * HD)
    return attended


def solution(mesh):
    torus = Mesh(mesh.devices.reshape(mesh.shape["ha"], 2, 4, 2), ("ha", "wa_0", "wa_1", "wa_2"))
    placed = (P("ha", WA, None, None), P("ha", WA, None, None, None, None), P(WA, "ha", None, None))
    return jax.shard_map(
        on_device, mesh=torus, in_specs=placed, out_specs=P("ha", WA, None, None), check_vma=False
    )
```

profile of v0, /device:TPU:25, one launch (start us, length us, event | category | flops | bytes accessed | tf_op | source)
XLA Modules:
  0.0 1148.8 jit_solution(3255809066478962625)
XLA Ops:
  0.0 7.8 collective-permute-start
  9.1 147.1 %collective-permute-done = bf16[1,1,3,2,384,1536]{5,4,3,2,1,0:T(8,128)(2,1)} collective-permute-done((bf16[1,1,3,2,384,1536]{5,4,3,2,1,0:T(8,128)(2,1)}, bf16[1,1,3,2,384,1536]{5,4,3,2,1,0:T(8,128)(2,1)}, u32[]{:S(2)}, u32[]{:S(2)}) %collective-permute-start) | collective-permute-done | bytes 7077920 | tf_op jit(solution)/shard_map/ppermute | solution.py:22
  156.3 6.7 constant_dynamic-update-slice_fusion.3
  163.0 3.3 constant_dynamic-update-slice_fusion.2
  166.3 143.9 %collective-permute-done.1 = bf16[1,1,3,2,384,1536]{5,4,3,2,1,0:T(8,128)(2,1)S(1)} collective-permute-done((bf16[1,1,3,2,384,1536]{5,4,3,2,1,0:T(8,128)(2,1)}, bf16[1,1,3,2,384,1536]{5,4,3,2,1,0:T(8,128)(2,1)S(1)}, u32[]{:S(2)}, u32[]{:S(2)}) %collective-permute-start.1) | collective-permute-done | bytes 7077920 | tf_op jit(solution)/shard_map/ppermute | solution.py:23
  310.1 3.4 constant_dynamic-update-slice_fusion.1
  313.5 3.4 collective-permute-start.3
  317.0 4.2 collective-permute-start.2
  322.1 28.6 %all_to_all.20 = s32[8,2,1,2]{0,3,2,1:T(2,128)S(1)} all-to-all(s32[8,2,1,2]{0,3,2,1:T(2,128)S(1)} %copy.50), channel_id=1, replica_groups=mesh['ha'=8,'wa_0'=2,'wa_1'=4,'wa_2'=2] {'wa_2'}, dimensions={1} | all-to-all | bytes 256 | tf_op jit(solution)/shard_map/all_to_all | solution.py:44
  351.4 12.1 %all-to-all-start.1 = ((s32[8,2,1,2]{1,3,2,0:T(2,128)}), s32[8,2,1,2]{1,3,2,0:T(2,128)S(1)}, u32[]{:S(2)}, u32[]{:S(2)}) async-start(s32[8,2,1,2]{1,3,2,0:T(2,128)} %copy.51), calls=%async_computation.1 | async-start | bytes 16384 | tf_op jit(solution)/shard_map/all_to_all | solution.py:44
  367.8 3.0 copy.57
  370.8 178.8 %all-to-all-done.1 = s32[8,2,1,2]{1,3,2,0:T(2,128)S(1)} async-done(((s32[8,2,1,2]{1,3,2,0:T(2,128)}), s32[8,2,1,2]{1,3,2,0:T(2,128)S(1)}, u32[]{:S(2)}, u32[]{:S(2)}) %all-to-all-start.1) | async-done | bytes 160 | tf_op jit(solution)/shard_map/all_to_all | solution.py:44
  550.4 4.0 gather_fusion
  554.5 3.2 copy.58
  557.7 8.4 all_to_all.21
  566.1 3.1 copy.59
  569.1 6.4 all-to-all-start.3
  576.2 69.0 %all-to-all-done.3 = bf16[8,2,1,2,2,384,128]{6,5,4,3,1,2,0:T(8,128)(2,1)} async-done(((bf16[8,2,1,2,2,384,128]{6,5,4,3,1,2,0:T(8,128)(2,1)}), bf16[8,2,1,2,2,384,128]{6,5,4,3,1,2,0:T(8,128)(2,1)}, u32[]{:S(2)}, u32[]{:S(2)}) %all-to-all-start.3) | async-done | bytes 6291488 | tf_op jit(solution)/shard_map/all_to_all | solution.py:44
  645.1 6.4 gather_fusion.1
  651.5 42.5 %pad_maximum_fusion.1 = bf16[3,3,3,2,384,1536]{5,4,3,2,1,0:T(8,128)(2,1)} fusion(bf16[3,1,3,2,384,1536]{5,4,3,2,1,0:T(8,128)(2,1)} %collective-permute-done.3, bf16[3,1,3,2,384,1536]{5,4,3,2,1,0:T(8,128)(2,1)} %constant_dynamic-update-slice_fusion.1, bf16[3,1,3,2,384,1536]{5,4,3,2,1,0:T(8,128)(2,1)} %collective-permute-done.2), kind=kLoop, calls=%fused_computation.29 | loop fusion | flops 63700992 | bytes 127401984 | tf_op jit(solution)/shard_map/concatenate | solution.py:24
  694.1 452.4 %while.10 = (s32[]{:T(128)}, bf16[12,1,384,128]{2,3,0,1:T(8,128)(2,1)}, pred[1,1,11136]{2,1,0:T(4,128)(4,1)S(1)}, s32[12]{0:T(128)S(1)}, bf16[1,384,1536]{2,1,0:...) while((s32[]{:T(128)}, ...), condition=%wide.region_6.7_spmd, body=%wide.region_3.6_spmd.sunk | while | flops 2236169472 | bytes 101687688 | solution.py:148
  696.4 2.9 dynamic-slice_bitcast_fusion.4
  701.9 12.3 %fusion.45 = (f32[384]{0:T(512)S(1)}, f32[384,11136]{1,0:T(8,128)}) fusion(bf16[1,768,128]{2,1,0:T(8,128)(2,1)S(1)} %bitcast.98, bf16[1,10368,128]{2,1,0:T(8,128)(2,1)S(1)} %bitcast.94, bf16[1,384,1536]{2,1,0:T(8,128)(2,1)} %get-tuple-element.189, s32[]{:T(128)S(6)} %select_n.162, pred[11136]{0:T(1024)(128)(4,1)S(1)} %reduce.6), kind=kOutput, calls=%fused_computation.75.clone.1 | convolution fusion | flops 1113243264 | bytes 20066692 | tf_op jit(solution)/shard_map/while/body/eval_jaxpr/iqd,ikd->iqk/dot_general | solution.py:133
  714.2 8.4 fusion.46
  722.6 8.4 fusion.47
  734.1 2.9 dynamic-slice_bitcast_fusion.4
  739.6 12.3 %fusion.45 = (f32[384]{0:T(512)S(1)}, f32[384,11136]{1,0:T(8,128)}) fusion(bf16[1,768,128]{2,1,0:T(8,128)(2,1)S(1)} %bitcast.98, bf16[1,10368,128]{2,1,0:T(8,128)(2,1)S(1)} %bitcast.94, bf16[1,384,1536]{2,1,0:T(8,128)(2,1)} %get-tuple-element.189, s32[]{:T(128)S(6)} %select_n.162, pred[11136]{0:T(1024)(128)(4,1)S(1)} %reduce.6), kind=kOutput, calls=%fused_computation.75.clone.1 | convolution fusion | flops 1113243264 | bytes 20066692 | tf_op jit(solution)/shard_map/while/body/eval_jaxpr/iqd,ikd->iqk/dot_general | solution.py:133
  751.9 8.4 fusion.46
  760.3 8.4 fusion.47
  777.3 12.3 %fusion.45 = (f32[384]{0:T(512)S(1)}, f32[384,11136]{1,0:T(8,128)}) fusion(bf16[1,768,128]{2,1,0:T(8,128)(2,1)S(1)} %bitcast.98, bf16[1,10368,128]{2,1,0:T(8,128)(2,1)S(1)} %bitcast.94, bf16[1,384,1536]{2,1,0:T(8,128)(2,1)} %get-tuple-element.189, s32[]{:T(128)S(6)} %select_n.162, pred[11136]{0:T(1024)(128)(4,1)S(1)} %reduce.6), kind=kOutput, calls=%fused_computation.75.clone.1 | convolution fusion | flops 1113243264 | bytes 20066692 | tf_op jit(solution)/shard_map/while/body/eval_jaxpr/iqd,ikd->iqk/dot_general | solution.py:133
  789.6 8.4 fusion.46
  798.0 8.4 fusion.47
  809.5 2.9 dynamic-slice_bitcast_fusion.4
  815.0 12.3 %fusion.45 = (f32[384]{0:T(512)S(1)}, f32[384,11136]{1,0:T(8,128)}) fusion(bf16[1,768,128]{2,1,0:T(8,128)(2,1)S(1)} %bitcast.98, bf16[1,10368,128]{2,1,0:T(8,128)(2,1)S(1)} %bitcast.94, bf16[1,384,1536]{2,1,0:T(8,128)(2,1)} %get-tuple-element.189, s32[]{:T(128)S(6)} %select_n.162, pred[11136]{0:T(1024)(128)(4,1)S(1)} %reduce.6), kind=kOutput, calls=%fused_computation.75.clone.1 | convolution fusion | flops 1113243264 | bytes 20066692 | tf_op jit(solution)/shard_map/while/body/eval_jaxpr/iqd,ikd->iqk/dot_general | solution.py:133
  827.3 8.4 fusion.46
  835.7 8.4 fusion.47
  852.7 12.3 %fusion.45 = (f32[384]{0:T(512)S(1)}, f32[384,11136]{1,0:T(8,128)}) fusion(bf16[1,768,128]{2,1,0:T(8,128)(2,1)S(1)} %bitcast.98, bf16[1,10368,128]{2,1,0:T(8,128)(2,1)S(1)} %bitcast.94, bf16[1,384,1536]{2,1,0:T(8,128)(2,1)} %get-tuple-element.189, s32[]{:T(128)S(6)} %select_n.162, pred[11136]{0:T(1024)(128)(4,1)S(1)} %reduce.6), kind=kOutput, calls=%fused_computation.75.clone.1 | convolution fusion | flops 1113243264 | bytes 20066692 | tf_op jit(solution)/shard_map/while/body/eval_jaxpr/iqd,ikd->iqk/dot_general | solution.py:133
  865.0 8.4 fusion.46
  873.4 8.4 fusion.47
  884.8 2.9 dynamic-slice_bitcast_fusion.4
  890.4 12.3 %fusion.45 = (f32[384]{0:T(512)S(1)}, f32[384,11136]{1,0:T(8,128)}) fusion(bf16[1,768,128]{2,1,0:T(8,128)(2,1)S(1)} %bitcast.98, bf16[1,10368,128]{2,1,0:T(8,128)(2,1)S(1)} %bitcast.94, bf16[1,384,1536]{2,1,0:T(8,128)(2,1)} %get-tuple-element.189, s32[]{:T(128)S(6)} %select_n.162, pred[11136]{0:T(1024)(128)(4,1)S(1)} %reduce.6), kind=kOutput, calls=%fused_computation.75.clone.1 | convolution fusion | flops 1113243264 | bytes 20066692 | tf_op jit(solution)/shard_map/while/body/eval_jaxpr/iqd,ikd->iqk/dot_general | solution.py:133
  902.6 8.4 fusion.46
  911.0 8.4 fusion.47
  922.5 2.9 dynamic-slice_bitcast_fusion.4
  928.1 12.3 %fusion.45 = (f32[384]{0:T(512)S(1)}, f32[384,11136]{1,0:T(8,128)}) fusion(bf16[1,768,128]{2,1,0:T(8,128)(2,1)S(1)} %bitcast.98, bf16[1,10368,128]{2,1,0:T(8,128)(2,1)S(1)} %bitcast.94, bf16[1,384,1536]{2,1,0:T(8,128)(2,1)} %get-tuple-element.189, s32[]{:T(128)S(6)} %select_n.162, pred[11136]{0:T(1024)(128)(4,1)S(1)} %reduce.6), kind=kOutput, calls=%fused_computation.75.clone.1 | convolution fusion | flops 1113243264 | bytes 20066692 | tf_op jit(solution)/shard_map/while/body/eval_jaxpr/iqd,ikd->iqk/dot_general | solution.py:133
  940.3 8.4 fusion.46
  948.7 8.4 fusion.47
  965.7 12.3 %fusion.45 = (f32[384]{0:T(512)S(1)}, f32[384,11136]{1,0:T(8,128)}) fusion(bf16[1,768,128]{2,1,0:T(8,128)(2,1)S(1)} %bitcast.98, bf16[1,10368,128]{2,1,0:T(8,128)(2,1)S(1)} %bitcast.94, bf16[1,384,1536]{2,1,0:T(8,128)(2,1)} %get-tuple-element.189, s32[]{:T(128)S(6)} %select_n.162, pred[11136]{0:T(1024)(128)(4,1)S(1)} %reduce.6), kind=kOutput, calls=%fused_computation.75.clone.1 | convolution fusion | flops 1113243264 | bytes 20066692 | tf_op jit(solution)/shard_map/while/body/eval_jaxpr/iqd,ikd->iqk/dot_general | solution.py:133
  978.0 8.4 fusion.46
  986.4 8.4 fusion.47
  997.9 2.9 dynamic-slice_bitcast_fusion.4
  1003.4 12.3 %fusion.45 = (f32[384]{0:T(512)S(1)}, f32[384,11136]{1,0:T(8,128)}) fusion(bf16[1,768,128]{2,1,0:T(8,128)(2,1)S(1)} %bitcast.98, bf16[1,10368,128]{2,1,0:T(8,128)(2,1)S(1)} %bitcast.94, bf16[1,384,1536]{2,1,0:T(8,128)(2,1)} %get-tuple-element.189, s32[]{:T(128)S(6)} %select_n.162, pred[11136]{0:T(1024)(128)(4,1)S(1)} %reduce.6), kind=kOutput, calls=%fused_computation.75.clone.1 | convolution fusion | flops 1113243264 | bytes 20066692 | tf_op jit(solution)/shard_map/while/body/eval_jaxpr/iqd,ikd->iqk/dot_general | solution.py:133
  1015.7 8.4 fusion.46
  1024.1 8.4 fusion.47
  1041.1 12.3 %fusion.45 = (f32[384]{0:T(512)S(1)}, f32[384,11136]{1,0:T(8,128)}) fusion(bf16[1,768,128]{2,1,0:T(8,128)(2,1)S(1)} %bitcast.98, bf16[1,10368,128]{2,1,0:T(8,128)(2,1)S(1)} %bitcast.94, bf16[1,384,1536]{2,1,0:T(8,128)(2,1)} %get-tuple-element.189, s32[]{:T(128)S(6)} %select_n.162, pred[11136]{0:T(1024)(128)(4,1)S(1)} %reduce.6), kind=kOutput, calls=%fused_computation.75.clone.1 | convolution fusion | flops 1113243264 | bytes 20066692 | tf_op jit(solution)/shard_map/while/body/eval_jaxpr/iqd,ikd->iqk/dot_general | solution.py:133
  1053.4 8.4 fusion.46
  1061.8 8.4 fusion.47
  1078.8 12.3 %fusion.45 = (f32[384]{0:T(512)S(1)}, f32[384,11136]{1,0:T(8,128)}) fusion(bf16[1,768,128]{2,1,0:T(8,128)(2,1)S(1)} %bitcast.98, bf16[1,10368,128]{2,1,0:T(8,128)(2,1)S(1)} %bitcast.94, bf16[1,384,1536]{2,1,0:T(8,128)(2,1)} %get-tuple-element.189, s32[]{:T(128)S(6)} %select_n.162, pred[11136]{0:T(1024)(128)(4,1)S(1)} %reduce.6), kind=kOutput, calls=%fused_computation.75.clone.1 | convolution fusion | flops 1113243264 | bytes 20066692 | tf_op jit(solution)/shard_map/while/body/eval_jaxpr/iqd,ikd->iqk/dot_general | solution.py:133
  1091.1 8.4 fusion.46
  1099.5 8.4 fusion.47
  1111.0 3.0 dynamic-slice_bitcast_fusion.4
  1116.6 12.3 %fusion.45 = (f32[384]{0:T(512)S(1)}, f32[384,11136]{1,0:T(8,128)}) fusion(bf16[1,768,128]{2,1,0:T(8,128)(2,1)S(1)} %bitcast.98, bf16[1,10368,128]{2,1,0:T(8,128)(2,1)S(1)} %bitcast.94, bf16[1,384,1536]{2,1,0:T(8,128)(2,1)} %get-tuple-element.189, s32[]{:T(128)S(6)} %select_n.162, pred[11136]{0:T(1024)(128)(4,1)S(1)} %reduce.6), kind=kOutput, calls=%fused_computation.75.clone.1 | convolution fusion | flops 1113243264 | bytes 20066692 | tf_op jit(solution)/shard_map/while/body/eval_jaxpr/iqd,ikd->iqk/dot_general | solution.py:133
  1128.9 8.4 fusion.46
  1137.3 8.4 fusion.47
  (176 shorter events, 85.9 us)
Async XLA Ops:
  0.0 163.0 %copy-start.1 = (bf16[1,1,3,2,384,1536]{5,4,3,2,1,0:T(8,128)(2,1)S(1)}, bf16[1,1,3,2,384,1536]{5,4,3,2,1,0:T(8,128)(2,1)}, u32[]{:S(2)}) copy-start(bf16[1,1,3,2,384,1536]{5,4,3,2,1,0:T(8,128)(2,1)} %param.6) | copy-start | bytes 21233668
  0.0 156.3 %collective-permute-start = (bf16[1,1,3,2,384,1536]{5,4,3,2,1,0:T(8,128)(2,1)}, bf16[1,1,3,2,384,1536]{5,4,3,2,1,0:T(8,128)(2,1)}, u32[]{:S(2)}, u32[]{:S(2)}) collective-permute-start(bf16[1,1,3,2,384,1536]{5,4,3,2,1,0:T(8,128)(2,1)} %param.6), channel_id=1, source_target_pairs={{0,16},{16,32},{32,48},{48,64},{64,80},{80,96},{96,112},{1,17},{17... | collective-permute-start | bytes 21233672 | tf_op jit(solution)/shard_map/ppermute | solution.py:22
  7.8 302.3 %collective-permute-start.1 = (bf16[1,1,3,2,384,1536]{5,4,3,2,1,0:T(8,128)(2,1)}, bf16[1,1,3,2,384,1536]{5,4,3,2,1,0:T(8,128)(2,1)S(1)}, u32[]{:S(2)}, u32[]{:S(2)}) collective-permute-start(bf16[1,1,3,2,384,1536]{5,4,3,2,1,0:T(8,128)(2,1)} %param.6), channel_id=1, source_target_pairs={{16,0},{32,16},{48,32},{64,48},{80,64},{96,80},{112,96},{17,1},{33... | collective-permute-start | bytes 21233672 | tf_op jit(solution)/shard_map/ppermute | solution.py:23
  166.3 154.9 %copy-start.2 = (s32[1,1,12,2]{2,3,1,0:T(2,128)S(1)}, s32[1,1,12,2]{2,3,1,0:T(2,128)}, u32[]{:S(2)}) copy-start(s32[1,1,12,2]{2,3,1,0:T(2,128)} %param.7) | copy-start | bytes 292
  313.5 338.0 %collective-permute-start.3 = (bf16[3,1,3,2,384,1536]{5,4,3,2,1,0:T(8,128)(2,1)}, bf16[3,1,3,2,384,1536]{5,4,3,2,1,0:T(8,128)(2,1)}, u32[]{:S(2)}, u32[]{:S(2)}) collective-permute-start(bf16[3,1,3,2,384,1536]{5,4,3,2,1,0:T(8,128)(2,1)} %constant_dynamic-update-slice_fusion.1), channel_id=1, source_target_pairs={{1,0},{2,1},{3,2},{4,3},{5,4},{6,5},{7,6},{8,7},{9,8},{10,9},{11,1... | collective-permute-start | bytes 63701000 | tf_op jit(solution)/shard_map/ppermute | solution.py:23
  317.0 334.5 %collective-permute-start.2 = (bf16[3,1,3,2,384,1536]{5,4,3,2,1,0:T(8,128)(2,1)}, bf16[3,1,3,2,384,1536]{5,4,3,2,1,0:T(8,128)(2,1)}, u32[]{:S(2)}, u32[]{:S(2)}) collective-permute-start(bf16[3,1,3,2,384,1536]{5,4,3,2,1,0:T(8,128)(2,1)} %constant_dynamic-update-slice_fusion.1), channel_id=1, source_target_pairs={{0,1},{1,2},{2,3},{3,4},{4,5},{5,6},{6,7},{7,8},{8,9},{9,10},{10,1... | collective-permute-start | bytes 63701000 | tf_op jit(solution)/shard_map/ppermute | solution.py:22
  351.4 198.2 %all-to-all-start.1 = ((s32[8,2,1,2]{1,3,2,0:T(2,128)}), s32[8,2,1,2]{1,3,2,0:T(2,128)S(1)}, u32[]{:S(2)}, u32[]{:S(2)}) async-start(s32[8,2,1,2]{1,3,2,0:T(2,128)} %copy.51), calls=%async_computation.1 | async-start | bytes 16384 | tf_op jit(solution)/shard_map/all_to_all | solution.py:44
  569.1 76.0 %all-to-all-start.3 = ((bf16[8,2,1,2,2,384,128]{6,5,4,3,1,2,0:T(8,128)(2,1)}), bf16[8,2,1,2,2,384,128]{6,5,4,3,1,2,0:T(8,128)(2,1)}, u32[]{:S(2)}, u32[]{:S(2)}) async-start(bf16[8,2,1,2,2,384,128]{6,5,4,3,1,2,0:T(8,128)(2,1)} %copy.59), calls=%async_computation.3 | async-start | bytes 12582912 | tf_op jit(solution)/shard_map/all_to_all | solution.py:44
  714.2 8.4 copy-start
  751.9 8.4 copy-start
  789.6 8.4 copy-start
  827.3 8.4 copy-start
  865.0 8.4 copy-start
  902.6 8.4 copy-start
  940.3 8.4 copy-start
  978.0 8.4 copy-start
  1015.7 8.4 copy-start
  1053.4 8.4 copy-start
  1091.1 8.4 copy-start
  1128.8 8.4 copy-start
where the time goes:
time: 1150 us
  waiting for transfers between devices  539 us (47%)
  matrix products  248 us (22%)
  other arithmetic  153 us (13%)
  local copies, waits for them, and re-layouts  129 us (11%)
  blocking collectives  37 us (3%)
  starting transfers between devices  35.3 us (3%)
    all_to_all x2, waiting for transfers between devices, moved_by_axis(): lax.all_to_all(blocks, axes[k], split_axis=k, concat_axis=k, tiled=True)  248 us
    dot_general x12, matrix products, one_head(): jnp.einsum('iqd,ikd->iqk', head_queries, key_tiles, preferred_element_typ...  147 us
    ppermute x2, waiting for transfers between devices, with_halo(): before = lax.ppermute(last, axis, up)  147 us
    ppermute x2, waiting for transfers between devices, with_halo(): after = lax.ppermute(first, axis, down)  144 us
    reduce_sum x12, other arithmetic, one_head(): totals = jnp.sum(weights, axis=2, keepdims=True)  101 us
    dot_general x12, matrix products, one_head(): jnp.einsum('iqk,ikd->iqd', weights.astype(jnp.bfloat16), value_tiles, pre...  100 us
    concatenate x1, other arithmetic, with_halo(): array = jnp.concatenate([before, array, after], axis=dim)  42.5 us
    all_to_all x2, blocking collectives, moved_by_axis(): lax.all_to_all(blocks, axes[k], split_axis=k, concat_axis=k, tiled=True)  37 us
  transfers between devices with their start and end apart: 6, of which 4 were waited for; matrix products, arithmetic and copies ran while one was open for 3% of the time, Pallas kernels for 0%

commit v1 on v0

v1 whole, which is shorter than its diff:
```python
import jax
import jax.numpy as jnp
from jax import lax
from jax.experimental import pallas as pl
from jax.experimental.pallas import tpu as pltpu
from jax.sharding import PartitionSpec as P

HEADS = 12
HD = 128
TILE = 384
TT = 3
FAR = 2
CAP = 2
NC = 3
HC = HEADS // NC
CW = HC * HD
TO_LOG2 = 1.4426950408889634 / HD**0.5
MESH = pl.DeviceIdType.MESH


def pack_far(off_ref, q_ref, slot_ref, qf_ref, qt_ref, heads, count):
    spans = qf_ref.shape[0] // CAP

    def clear(i, carry):
        heads[i] = 0
        count[i] = 0
        return carry

    lax.fori_loop(0, spans * CAP, clear, 0)
    qf_ref[...] = jnp.zeros_like(qf_ref)

    def place(i, carry):
        offset = off_ref[i]
        taken = count[offset]
        count[offset] = taken + 1
        slot = offset * CAP + jnp.minimum(taken, CAP - 1)
        head = i // FAR
        slot_ref[i] = slot
        heads[slot] = head
        qf_ref[slot] = q_ref[:, pl.ds(pl.multiple_of(head * HD, HD), HD)]
        return carry

    lax.fori_loop(0, HEADS * FAR, place, 0)
    lane = lax.broadcasted_iota(jnp.int32, (8, HD), 1)
    for s in range(spans):
        qt_ref[s] = jnp.where(lane == 0, heads[s * CAP], heads[s * CAP + 1])


def attend(q, k, v_one):
    s = lax.dot_general(q, k, (((1,), (1,)), ((), ())), preferred_element_type=jnp.float32)
    peak = jnp.max(s, axis=1, keepdims=True)
    p = jnp.exp2(s * TO_LOG2 - peak * TO_LOG2)
    both = jnp.dot(p.astype(jnp.bfloat16), v_one, preferred_element_type=jnp.float32)
    total = both[:, HD:]
    return (both[:, :HD] * (1.0 / total)).astype(jnp.bfloat16), peak * TO_LOG2 + jnp.log2(total)


def with_ones(v):
    return jnp.concatenate([v, jnp.ones(v.shape, v.dtype)], axis=1)


def blend_weights(rows):
    peak = rows[0]
    for row in rows[1:]:
        peak = jnp.maximum(peak, row)
    parts = [jnp.exp2(row - peak) for row in rows]
    total = parts[0]
    for part in parts[1:]:
        total = total + part
    inverse = 1.0 / total
    stack = [part * inverse for part in parts]
    stack.append(jnp.zeros((HD - 8 * len(rows), TILE), jnp.float32))
    return jnp.transpose(jnp.concatenate(stack, axis=0)), peak + jnp.log2(total)


def fused(
    spans, rows_ha, cols_wa, slot_ref, q_ref, kv_ref, qf_ref, qt_ref, out_ref,
    QW, KV, O, LO, OI, LI, ZS, ZL, ZI, ZLI, XS, XL, XI, XLI, FQ, TI, TS, FO, FL, FI, FLI, FLX, AC,
    kv_sem, q_sem, t_sem, v_s, v_r, z_s, z_r, h_s, h_r, o_s, o_r, l_s, l_r,
    zo_s, zo_r, zl_s, zl_r, xo_s, xo_r, xl_s, xl_r, fq_s, fq_r, ft_s, ft_r, fo_s, fo_r, fl_s, fl_r,
):
    h = lax.axis_index("ha")
    w = lax.axis_index("wa")
    sign = 1 - 2 * (h % 2)
    partner = h + sign
    z_to = (h + 2 * sign + rows_ha) % rows_ha
    z_from = (h - 2 * sign + rows_ha) % rows_ha
    left = (w + cols_wa - 1) % cols_wa
    right = (w + 1) % cols_wa
    has_left = w > 0
    has_right = w < cols_wa - 1
    has_far_row = (h + 2 * sign >= 0) & (h + 2 * sign < rows_ha)

    def cols_of(c):
        return pl.ds(pl.multiple_of(c * CW, CW), CW)

    def remote(src, dst, ss, rs, ha=None, wa=None):
        return pltpu.make_async_remote_copy(
            src_ref=src, dst_ref=dst, send_sem=ss, recv_sem=rs,
            device_id={"ha": h if ha is None else ha, "wa": w if wa is None else wa},
            device_id_type=MESH,
        )

    def kv_in(c):
        cols = pl.ds(pl.multiple_of(c * HD, HD), HD)
        return pltpu.make_async_copy(kv_ref.at[:, :, :, cols], KV.at[c], kv_sem.at[c])

    def q_in(c):
        return pltpu.make_async_copy(q_ref.at[:, cols_of(c)], QW.at[0, c], q_sem.at[c])

    def send_v(c):
        return remote(q_ref.at[:, cols_of(c)], QW.at[3, c], v_s.at[c], v_r.at[c], ha=partner)

    def send_z(c):
        return remote(QW.at[3, c], QW.at[6, c], z_s.at[c], z_r.at[c], ha=z_to)

    def send_h(r, side, c):
        src = q_ref.at[:, cols_of(c)] if r == 0 else QW.at[3 * r, c]
        i = r * 2 + side
        return remote(
            src, QW.at[3 * r + 2 - side, c], h_s.at[i, c], h_r.at[i, c],
            wa=right if side else left,
        )

    def send_o(r, side, c):
        i = r * 2 + side
        return (
            remote(O.at[3 * r + 1 + side, c], OI.at[r * 2 + 1 - side, c], o_s.at[i, c], o_r.at[i, c],
                   wa=right if side else left),
            remote(LO.at[3 * r + 1 + side, c], LI.at[r * 2 + 1 - side, c], l_s.at[i, c], l_r.at[i, c],
                   wa=right if side else left),
        )

    def send_zo(c):
        return (
            remote(ZS.at[c], ZI.at[c], zo_s.at[c], zo_r.at[c], ha=z_from),
            remote(ZL.at[c], ZLI.at[c], zl_s.at[c], zl_r.at[c], ha=z_from),
        )

    def send_xo(c):
        return (
            remote(XS.at[c], XI.at[c], xo_s.at[c], xo_r.at[c], ha=partner),
            remote(XL.at[c], XLI.at[c], xl_s.at[c], xl_r.at[c], ha=partner),
        )

    def send_fq(s):
        owner = (w + 1 + s) % cols_wa
        return (
            remote(qt_ref.at[s], TI.at[s], ft_s.at[s], ft_r.at[s], wa=owner),
            remote(qf_ref.at[pl.ds(s * CAP, CAP)], FQ.at[pl.ds(s * CAP, CAP)], fq_s.at[s], fq_r.at[s], wa=owner),
        )

    def send_fo(s):
        asker = (w + 2 * cols_wa - 1 - s) % cols_wa
        return (
            remote(FO.at[pl.ds(s * CAP, CAP)], FI.at[pl.ds(s * CAP, CAP)], fo_s.at[s], fo_r.at[s], wa=asker),
            remote(FL.at[s], FLI.at[s], fl_s.at[s], fl_r.at[s], wa=asker),
        )

    def chunks(step):
        def run(c, carry):
            step(c)
            return carry

        lax.fori_loop(0, NC, run, 0)

    def kv_start(head, carry):
        kv_in(head).start()
        return carry

    lax.fori_loop(0, HEADS, kv_start, 0)

    @chunks
    def _(c):
        q_in(c).start()
        send_v(c).start()

    @chunks
    def _(c):
        send_h(0, 0, c).start()
        send_h(0, 1, c).start()

    def far_out(s, carry):
        for copy in send_fq(s):
            copy.start()
        return carry

    lax.fori_loop(0, spans, far_out, 0)

    AC[...] = jnp.zeros_like(AC)
    lane = lax.broadcasted_iota(jnp.int32, (TILE, HD), 1)

    def head_cols(hh):
        return pl.ds(pl.multiple_of(hh * HD, HD), HD)

    def keys_values_of(head):
        k = KV[head, :, 0].reshape(TT * TILE, HD)
        v = KV[head, :, 1].reshape(TT * TILE, HD)
        return k, with_ones(v)

    def pair(a, b, c):
        def step(hh, carry):
            cols = head_cols(hh)
            k, v = keys_values_of(c * HC + hh)
            for i, slot in enumerate((a, b)):
                o, l = attend(QW[slot, c, :, cols], k, v)
                O[slot, c, :, cols] = o
                AC[i] = jnp.where(lane == hh, l, AC[i])
            return carry

        lax.fori_loop(0, HC, step, 0)
        for i, slot in enumerate((a, b)):
            LO[slot, c] = jnp.transpose(AC[i])[:8]

    @chunks
    def _(c):
        for hh in range(HC):
            kv_in(c * HC + hh).wait()
        q_in(c).wait()

        def step(half, carry):
            for e in range(2):
                hh = half * 2 + e
                cols = head_cols(hh)
                k, v = keys_values_of(c * HC + hh)
                o, l = attend(QW[0, c, :, cols], k, v)
                O[0, c, :, cols] = o
                AC[0] = jnp.where(lane == hh, l, AC[0])
            return carry

        lax.fori_loop(0, HC // 2, step, 0)
        LO[0, c] = jnp.transpose(AC[0])[:8]

    def give_back(r, c):
        for side in range(2):
            for copy in send_o(r, side, c):
                copy.start()

    @chunks
    def _(c):
        send_h(0, 0, c).wait_recv()
        send_h(0, 1, c).wait_recv()
        pair(1, 2, c)
        give_back(0, c)
        send_v(c).wait_recv()
        send_z(c).start()
        send_h(1, 0, c).start()
        send_h(1, 1, c).start()

    @chunks
    def _(c):
        send_z(c).wait_recv()
        send_h(2, 0, c).start()
        send_h(2, 1, c).start()
        pair(3, 6, c)

    def far_step(s, carry):
        for copy in send_fq(s):
            copy.wait_recv()
        table = pltpu.make_async_copy(TI.at[s], TS, t_sem)
        table.start()
        table.wait()
        for p in range(CAP):
            head = TS[0, p]
            o, l = attend(FQ[s * CAP + p], KV[head, 1, 0], with_ones(KV[head, 1, 1]))
            FO[s * CAP + p] = o
            AC[0] = jnp.where(lane == p, l, AC[0])
        FL[s] = jnp.transpose(AC[0])[:8]
        for copy in send_fo(s):
            copy.start()
        return carry

    lax.fori_loop(0, spans, far_step, 0)

    for r in (2, 1):

        @chunks
        def _(c):
            send_h(r, 0, c).wait_recv()
            send_h(r, 1, c).wait_recv()
            pair(3 * r + 1, 3 * r + 2, c)
            give_back(r, c)

    def arrived(r, c):
        for side in range(2):
            for copy in send_o(r, side, c):
                copy.wait_recv()

    def masked(row, ok):
        return jnp.where(ok, row, -1e30)

    def row_parts(r, c):
        outs = [O.at[3 * r, c], OI.at[2 * r, c], OI.at[2 * r + 1, c]]
        rows = [LO[3 * r, c], masked(LI[2 * r, c], has_left), masked(LI[2 * r + 1, c], has_right)]
        return outs, rows

    def blend(outs, weights, hh):
        total = None
        for i, o in enumerate(outs):
            term = o.astype(jnp.float32) * weights[:, i * 8 + hh : i * 8 + hh + 1]
            total = term if total is None else total + term
        return total.astype(jnp.bfloat16)

    @chunks
    def _(c):
        arrived(2, c)
        outs, rows = row_parts(2, c)
        weights, joint = blend_weights(rows)
        ZL[c] = joint
        for hh in range(HC):
            cols = slice(hh * HD, (hh + 1) * HD)
            ZS[c, :, cols] = blend([o[:, cols] for o in outs], weights, hh)
        for copy in send_zo(c):
            copy.start()

    @chunks
    def _(c):
        arrived(1, c)
        for copy in send_zo(c):
            copy.wait_recv()
        outs, rows = row_parts(1, c)
        outs.append(ZI.at[c])
        rows.append(masked(ZLI[c], has_far_row))
        weights, joint = blend_weights(rows)
        XL[c] = joint
        for hh in range(HC):
            cols = slice(hh * HD, (hh + 1) * HD)
            XS[c, :, cols] = blend([o[:, cols] for o in outs], weights, hh)
        for copy in send_xo(c):
            copy.start()

    def far_in(s, carry):
        for copy in send_fo(s):
            copy.wait_recv()
        for p in range(CAP):
            FLX[s * CAP + p] = FLI[s, p : p + 1, :]
        return carry

    lax.fori_loop(0, spans, far_in, 0)

    @chunks
    def _(c):
        arrived(0, c)
        for copy in send_xo(c):
            copy.wait_recv()
        outs, rows = row_parts(0, c)
        outs.append(XI.at[c])
        rows.append(XLI[c])
        far = [[slot_ref[(c * HC + hh) * FAR + f] for hh in range(HC)] for f in range(FAR)]
        for f in range(FAR):
            lines = [FLX[slot] for slot in far[f]]
            lines.append(jnp.zeros((8 - HC, TILE), jnp.float32))
            rows.append(jnp.concatenate(lines, axis=0))
        weights, _joint = blend_weights(rows)
        for hh in range(HC):
            cols = slice(hh * HD, (hh + 1) * HD)
            values = [o[:, cols] for o in outs] + [FI[far[f][hh]] for f in range(FAR)]
            out_ref[:, pl.ds(pl.multiple_of(c * CW + hh * HD, HD), HD)] = blend(values, weights, hh)

    @chunks
    def _(c):
        send_v(c).wait_send()
        send_z(c).wait_send()
        for r in range(3):
            for side in range(2):
                send_h(r, side, c).wait_send()
                for copy in send_o(r, side, c):
                    copy.wait_send()
        for copy in send_zo(c) + send_xo(c):
            copy.wait_send()

    def far_done(s, carry):
        for copy in send_fq(s) + send_fo(s):
            copy.wait_send()
        return carry

    lax.fori_loop(0, spans, far_done, 0)


def solution(mesh):
    rows_ha, cols_wa = mesh.shape["ha"], mesh.shape["wa"]
    spans = cols_wa - 1
    bf16, f32 = jnp.bfloat16, jnp.float32
    any_space = pl.BlockSpec(memory_space=pl.ANY)
    smem = pl.BlockSpec(memory_space=pltpu.SMEM)
    vmem = pl.BlockSpec(memory_space=pltpu.VMEM)

    def tiles(*lead):
        return pltpu.VMEM((*lead, TILE, CW), bf16)

    def lines(*lead):
        return pltpu.VMEM((*lead, 8, TILE), f32)

    def sems(*dims):
        return [pltpu.SemaphoreType.DMA(dims)] * 2

    def on_device(queries, keys_values, far_offsets):
        q = queries[0, 0]
        slots, qf, qt = pl.pallas_call(
            pack_far,
            out_shape=(
                jax.ShapeDtypeStruct((HEADS * FAR,), jnp.int32),
                jax.ShapeDtypeStruct((spans * CAP, TILE, HD), bf16),
                jax.ShapeDtypeStruct((spans, 8, HD), jnp.int32),
            ),
            in_specs=[smem, vmem],
            out_specs=(smem, vmem, vmem),
            scratch_shapes=[pltpu.SMEM((spans * CAP,), jnp.int32), pltpu.SMEM((spans * CAP,), jnp.int32)],
            name="pack_far",
        )(far_offsets.reshape(HEADS * FAR), q)
        out = pl.pallas_call(
            lambda *refs: fused(spans, rows_ha, cols_wa, *refs),
            out_shape=jax.ShapeDtypeStruct((TILE, HEADS * HD), bf16),
            in_specs=[smem, any_space, any_space, any_space, any_space],
            out_specs=vmem,
            scratch_shapes=[
                tiles(9, NC), pltpu.VMEM((HEADS, TT, 2, TILE, HD), bf16), tiles(9, NC), lines(9, NC),
                tiles(6, NC), lines(6, NC), tiles(NC), lines(NC), tiles(NC), lines(NC),
                tiles(NC), lines(NC), tiles(NC), lines(NC),
                pltpu.VMEM((spans * CAP, TILE, HD), bf16), pltpu.VMEM((spans, 8, HD), jnp.int32),
                pltpu.SMEM((8, HD), jnp.int32),
                pltpu.VMEM((spans * CAP, TILE, HD), bf16), lines(spans),
                pltpu.VMEM((spans * CAP, TILE, HD), bf16), lines(spans),
                pltpu.VMEM((spans * CAP, 1, TILE), f32), pltpu.VMEM((2, TILE, HD), f32),
                pltpu.SemaphoreType.DMA((HEADS,)), pltpu.SemaphoreType.DMA((NC,)), pltpu.SemaphoreType.DMA,
                *sems(NC), *sems(NC), *sems(6, NC), *sems(6, NC), *sems(6, NC),
                *sems(NC), *sems(NC), *sems(NC), *sems(NC),
                *sems(spans), *sems(spans), *sems(spans), *sems(spans),
            ],
            compiler_params=pltpu.CompilerParams(has_side_effects=True, vmem_limit_bytes=67043328),
            name="fused",
        )(slots, q, keys_values[0, 0], qf, qt)
        return out[None, None]

    placed = (
        P("ha", "wa", None, None),
        P("ha", "wa", None, None, None, None),
        P("wa", "ha", None, None),
    )
    return jax.shard_map(
        on_device, mesh=mesh, in_specs=placed, out_specs=P("ha", "wa", None, None), check_vma=False
    )
```

time: 1150 us -> 248 us (0.22)
  waiting for transfers between devices: 539 us -> 0 us
  matrix products: 248 us -> 0 us
  Pallas kernels: 0 us -> 244 us
  other arithmetic: 153 us -> 0 us
  local copies, waits for them, and re-layouts: 129 us -> 3.75 us
  blocking collectives: 37 us -> 0 us
  starting transfers between devices: 35.3 us -> 0 us
    ppermute x4 -> x0, waiting for transfers between devices: 291 us -> none  [the longest x2 147 us: with_halo(): before = lax.ppermute(last, axis, up)]
    all_to_all x2 -> x0, waiting for transfers between devices: 248 us -> none  [moved_by_axis(): lax.all_to_all(blocks, axes[k], split_axis=k, concat_axis=k, tiled=True)]
    dot_general x24 -> x0, matrix products: 248 us -> none  [the longest x12 147 us: one_head(): jnp.einsum('iqd,ikd->iqk', head_queries, key_tiles, preferred_element_typ...]
    pallas_call x0 -> x2, Pallas kernels: none -> 244 us  [the longest x1 240 us: on_device(): pl.pallas_call(lambda *refs: fused(spans, rows_ha, cols_wa, *refs), out_s...]
    reduce_sum x14 -> x0, other arithmetic: 101 us -> none  [the longest x12 101 us: one_head(): totals = jnp.sum(weights, axis=2, keepdims=True)]
    concatenate x3 -> x0, other arithmetic: 42.6 us -> none  [the longest x1 42.5 us: with_halo(): array = jnp.concatenate([before, array, after], axis=dim)]
    another operation x14 -> x0, local copies, waits for them, and re-layouts: 41.4 us -> none  [the longest x12 35.2 us: one_head(): jnp.stack([head_kv[row_step:row_step + tile_rows] for row_step in range(3...]
    all_to_all x2 -> x0, blocking collectives: 37 us -> none  [moved_by_axis(): lax.all_to_all(blocks, axes[k], split_axis=k, concat_axis=k, tiled=True)]
  transfers between devices with their start and end apart: 6 -> 0, of which waited for: 4 -> 0; matrix products, arithmetic and copies ran while one was open for 3% -> 0% of each run, Pallas kernels for 0% -> 0%
where the time goes in v1:
time: 248 us
  Pallas kernels  244 us (98%)
  local copies, waits for them, and re-layouts  3.75 us (2%)
    pallas_call x1, Pallas kernels, on_device(): pl.pallas_call(lambda *refs: fused(spans, rows_ha, cols_wa, *refs), out_s...  240 us

profile of v1, /device:TPU:25, one launch (start us, length us, event | category | flops | bytes accessed | tf_op | source)
XLA Modules:
  0.0 247.9 jit_solution(6824078389691001326)
XLA Ops:
  0.0 0.8 copy.5
  0.8 0.6 reshape.3.off_ref
  1.4 4.2 %pack_far.1 = (s32[24]{0:T(128)}, bf16[30,384,128]{2,1,0:T(8,128)(2,1)}, s32[15,8,128]{2,1,0:T(8,128)}) custom-call(s32[24]{0:T(128)} %reshape.3.off_ref, bf16[384,1536]{1,0:T(8,128)(2,1)} %bitcast.4), custom_call_target="tpu_custom_call" | custom-call | tf_op jit(solution)/shard_map/pack_far/pallas_call | solution.py:399
  5.6 240.0 %fused.1 = bf16[384,1536]{1,0:T(8,128)(2,1)} custom-call(s32[24]{0:T(128)} %get-tuple-element.8.refs_0_, bf16[384,1536]{1,0:T(8,128)(2,1)} %bitcast.5, bf16[3,2,384,1536]{3,2,1,0:T(8,128)(2,1)} %bitcast.3, bf16[30,384,128]{2,1,0:T(8,128)(2,1)} %get-tuple-element.9.refs_3_, s32[15,8,128]{2,1,0:T(8,128)} %get-tuple-element.10.refs_4_), custom_call_target="tpu_custom_call" | custom-call | tf_op jit(solution)/shard_map/fused/pallas_call | solution.py:411
  245.6 2.4 copy.7

commit v2 on v1

--- a/solution.py
+++ b/solution.py
@@ -180,8 +180,8 @@
         send_h(0, 0, c).start()
         send_h(0, 1, c).start()
 
-    def far_out(s, carry):
-        for copy in send_fq(s):
+    def far_out(k, carry):
+        for copy in send_fq(k * 4 % spans):
             copy.start()
         return carry
 
@@ -254,7 +254,8 @@
         send_h(2, 1, c).start()
         pair(3, 6, c)
 
-    def far_step(s, carry):
+    def far_step(k, carry):
+        s = k * 4 % spans
         for copy in send_fq(s):
             copy.wait_recv()
         table = pltpu.make_async_copy(TI.at[s], TS, t_sem)

time: 248 us -> 238 us (0.960)
  Pallas kernels: 244 us -> 234 us
    pallas_call x1, Pallas kernels: 240 us -> 230 us  [on_device(): pl.pallas_call(lambda *refs: fused(spans, rows_ha, cols_wa, *refs), out_s...]
where the time goes in v2:
time: 238 us
  Pallas kernels  234 us (98%)
  local copies, waits for them, and re-layouts  3.75 us (2%)
    pallas_call x1, Pallas kernels, on_device(): pl.pallas_call(lambda *refs: fused(spans, rows_ha, cols_wa, *refs), out_s...  230 us

profile of v2, /device:TPU:25, one launch (start us, length us, event | category | flops | bytes accessed | tf_op | source)
XLA Modules:
  0.0 237.7 jit_solution(16893005736247119921)
XLA Ops:
  0.0 0.8 copy.5
  0.8 0.6 reshape.3.off_ref
  1.4 4.2 %pack_far.1 = (s32[24]{0:T(128)}, bf16[30,384,128]{2,1,0:T(8,128)(2,1)}, s32[15,8,128]{2,1,0:T(8,128)}) custom-call(s32[24]{0:T(128)} %reshape.3.off_ref, bf16[384,1536]{1,0:T(8,128)(2,1)} %bitcast.4), custom_call_target="tpu_custom_call" | custom-call | tf_op jit(solution)/shard_map/pack_far/pallas_call | solution.py:400
  5.6 229.7 %fused.1 = bf16[384,1536]{1,0:T(8,128)(2,1)} custom-call(s32[24]{0:T(128)} %get-tuple-element.8.refs_0_, bf16[384,1536]{1,0:T(8,128)(2,1)} %bitcast.5, bf16[3,2,384,1536]{3,2,1,0:T(8,128)(2,1)} %bitcast.3, bf16[30,384,128]{2,1,0:T(8,128)(2,1)} %get-tuple-element.9.refs_3_, s32[15,8,128]{2,1,0:T(8,128)} %get-tuple-element.10.refs_4_), custom_call_target="tpu_custom_call" | custom-call | tf_op jit(solution)/shard_map/fused/pallas_call | solution.py:412
  235.3 2.4 copy.7

commit v3 on v2

--- a/solution.py
+++ b/solution.py
@@ -181,7 +181,7 @@
         send_h(0, 1, c).start()
 
     def far_out(k, carry):
-        for copy in send_fq(k * 4 % spans):
+        for copy in send_fq(k * 7 % spans):
             copy.start()
         return carry
 
@@ -255,7 +255,7 @@
         pair(3, 6, c)
 
     def far_step(k, carry):
-        s = k * 4 % spans
+        s = k * 7 % spans
         for copy in send_fq(s):
             copy.wait_recv()
         table = pltpu.make_async_copy(TI.at[s], TS, t_sem)

time: 238 us -> 239 us (level)
  no operation moved by 1% of the time
where the time goes in v3:
time: 239 us; the launch traced here: 238 us
  Pallas kernels  234 us (98%)
  local copies, waits for them, and re-layouts  3.75 us (2%)
    pallas_call x1, Pallas kernels, on_device(): pl.pallas_call(lambda *refs: fused(spans, rows_ha, cols_wa, *refs), out_s...  230 us

profile of v3, /device:TPU:25, one launch (start us, length us, event | category | flops | bytes accessed | tf_op | source)
XLA Modules:
  0.0 238.2 jit_solution(8525169311497166783)
XLA Ops:
  0.0 0.8 copy.5
  0.8 0.6 reshape.3.off_ref
  1.4 4.2 %pack_far.1 = (s32[24]{0:T(128)}, bf16[30,384,128]{2,1,0:T(8,128)(2,1)}, s32[15,8,128]{2,1,0:T(8,128)}) custom-call(s32[24]{0:T(128)} %reshape.3.off_ref, bf16[384,1536]{1,0:T(8,128)(2,1)} %bitcast.4), custom_call_target="tpu_custom_call" | custom-call | tf_op jit(solution)/shard_map/pack_far/pallas_call | solution.py:400
  5.6 230.2 %fused.1 = bf16[384,1536]{1,0:T(8,128)(2,1)} custom-call(s32[24]{0:T(128)} %get-tuple-element.8.refs_0_, bf16[384,1536]{1,0:T(8,128)(2,1)} %bitcast.5, bf16[3,2,384,1536]{3,2,1,0:T(8,128)(2,1)} %bitcast.3, bf16[30,384,128]{2,1,0:T(8,128)(2,1)} %get-tuple-element.9.refs_3_, s32[15,8,128]{2,1,0:T(8,128)} %get-tuple-element.10.refs_4_), custom_call_target="tpu_custom_call" | custom-call | tf_op jit(solution)/shard_map/fused/pallas_call | solution.py:412
  235.8 2.4 copy.7
